TPU v7x, 128 devices: a whole 4x4x4 slice. The times are simulated.
128 devices in a mesh: row: 8 (over z, core), col: 16 (over y, x).
Axes of the slice: x: 4, y: 4, z: 4, core: 2. Of those that a mesh axis runs over, the one named last changes fastest.
Arguments:
- kernel: float32 [16384, 16384], P('row', 'col'), may hold values from 0 to 3, as said below
Outputs:
- trailing: float32 [16384, 16384], P('row', 'col')
- factor_t: float32 [1024, 16384], P('col', 'row')
Inputs may be any that keep to these rules, and one draw needn't show every extreme that they name: K is symmetric: an RBF kernel over 256 donor features plus each donor's noise variance, of 0.5 or more, on the diagonal.
All inputs are finite; a program needn't handle non-finite values.
Results may differ from a plain program's by a relative error of at most 0.0003.
Values sent between devices are 32-bit elements; how exact they have to be, the bound alone decides.
A program may use at most 128 MiB of HBM per device.

v0:
```python
import jax
import jax.numpy as jnp
from jax import lax
from jax.sharding import PartitionSpec as P

PANEL = 512
PANELS = 2
TILE = 32
HIGHEST = lax.Precision.HIGHEST


def mm(a, b):
    return jnp.dot(a, b, precision=HIGHEST, preferred_element_type=jnp.float32)


def mm_tn(a, b):
    return lax.dot_general(
        a, b, (((0,), (0,)), ((), ())), precision=HIGHEST, preferred_element_type=jnp.float32
    )


def mm_nt(a, b):
    return lax.dot_general(
        a, b, (((1,), (1,)), ((), ())), precision=HIGHEST, preferred_element_type=jnp.float32
    )


def tri_inverse(lower):
    eye = jnp.eye(lower.shape[0], dtype=lower.dtype)
    return jax.scipy.linalg.solve_triangular(lower, eye, lower=True)


def sym_chol(block):
    return jnp.linalg.cholesky(block)


def local(kernel):
    grid_rows = lax.axis_size("row")
    grid_cols = lax.axis_size("col")
    my_row = lax.axis_index("row")
    my_col = lax.axis_index("col")
    rows_loc, cols_loc = kernel.shape
    lead = PANELS * PANEL
    lead_rt = lead // (TILE * grid_rows)
    lead_ct = lead // (TILE * grid_cols)
    lead_r = lead_rt * TILE
    lead_c = lead_ct * TILE
    row_local = jnp.arange(rows_loc, dtype=jnp.int32)
    row_ids = (row_local // TILE * grid_rows + my_row) * TILE + row_local % TILE
    col_local = jnp.arange(cols_loc, dtype=jnp.int32)
    col_ids = (col_local // TILE * grid_cols + my_col) * TILE + col_local % TILE
    corner = kernel[:lead_r, :lead_c].reshape(1, lead_r * lead_c)
    blocks = lax.all_gather(corner, ("row", "col"), axis=0, tiled=True)
    blocks = blocks.reshape(grid_rows, grid_cols, lead_rt, TILE, lead_ct, TILE)
    a_lead = blocks.transpose(2, 0, 3, 4, 1, 5).reshape(lead, lead)
    cols_part = lax.all_gather(kernel[:, :lead_c], "col", axis=1, tiled=True)
    cols_part = cols_part.reshape(rows_loc, grid_cols, lead_ct, TILE)
    x_rows = cols_part.transpose(0, 2, 1, 3).reshape(rows_loc, lead)
    rows_part = lax.all_gather(kernel[:lead_r, :], "row", axis=0, tiled=True)
    rows_part = rows_part.reshape(grid_rows, lead_rt, TILE, cols_loc)
    y_cols = rows_part.transpose(1, 0, 2, 3).reshape(lead, cols_loc)
    a00 = a_lead[:PANEL, :PANEL]
    a01 = a_lead[:PANEL, PANEL:]
    a11 = a_lead[PANEL:, PANEL:]
    l0 = sym_chol(a00)
    l0inv = tri_inverse(l0)
    g0p1 = mm(l0inv, a01)
    s11 = a11 - mm_tn(g0p1, g0p1)
    l1 = sym_chol(s11)
    l1inv = tri_inverse(l1)

    def factor(panel_t, ids):
        g0 = mm(l0inv, panel_t[:PANEL])
        s1 = panel_t[PANEL:] - mm_tn(g0p1, g0)
        g1 = mm(l1inv, s1)
        g1 = jnp.where(ids[None, :] >= PANEL, g1, 0.0)
        return jnp.concatenate([g0, g1], axis=0)

    g_rows = factor(x_rows.T, row_ids)
    g_cols = factor(y_cols, col_ids)
    schur = kernel - mm_tn(g_rows, g_cols)
    keep = (row_ids[:, None] >= lead) & (col_ids[None, :] >= lead)
    trailing = jnp.where(keep, schur, 0.0)
    per_col = lead // grid_cols
    factor_out = lax.dynamic_slice_in_dim(g_rows, my_col * per_col, per_col, 0)
    return (trailing, factor_out)


def solution(mesh):
    return jax.shard_map(
        local,
        mesh=mesh,
        in_specs=(P("row", "col"),),
        out_specs=(P("row", "col"), P("col", "row")),
        check_vma=False,
    )
```

profile of v0, /device:TPU:1, one launch (start us, length us, event | category | flops | bytes accessed | tf_op | source)
XLA Modules:
  0.0 584.9 jit_solution(12073595241916444088)
XLA Ops:
  12.2 34.1 %all-gather.7.cloned.1.call-done = f32[1024,1024]{1,0:T(8,128)} async-done(((f32[128,1024]{1,0:T(8,128)}), f32[1024,1024]{1,0:T(8,128)}) %all-gather.7.cloned.1.call-update) | async-done | bytes 4194320 | tf_op jit(solution)/shard_map/all_gather | solution.py:59
  51.7 65.0 %all-gather.9.cloned.1.call-done = f32[128,1,8192]{2,1,0:T(1,128)} async-done(((f32[1,1,8192]{2,1,0:T(1,128)}), f32[128,1,8192]{2,1,0:T(1,128)}) %all-gather.9.cloned.1.call-update) | async-done | bytes 4194320 | tf_op jit(solution)/shard_map/all_gather | solution.py:53
  116.7 13.2 %reduce.16 = f32[128,8192]{1,0:T(8,128)} reduce(f32[128,1,8192]{2,1,0:T(1,128)} %all-gather.9.cloned.1.call-done, f32[]{:T(128)} %constant.211), dimensions={1}, to_apply=%all-gather.reduce_sub_computation | reduce | bytes 8388612 | tf_op jit(solution)/shard_map/all_gather | solution.py:53
  129.9 16.6 %reshape.139 = f32[8,16,4,32,2,32]{5,4,3,2,1,0:T(2,128)} reshape(f32[128,8192]{1,0:T(8,128)} %reduce.16) | data formatting | bytes 8388608 | tf_op jit(solution)/shard_map/reshape | solution.py:54
  146.5 26.1 %copy.20 = f32[4,8,32,2,16,32]{2,1,0,5,4,3:T(8,128)} copy(f32[4,8,32,2,16,32]{5,3,2,0,4,1:T(2,128)} %bitcast.121) | data formatting | bytes 8388608 | tf_op jit(solution)/shard_map/transpose | solution.py:55
  172.6 14.3 %reshape.140 = f32[1024,1024]{0,1:T(8,128)} reshape(f32[4,8,32,2,16,32]{2,1,0,5,4,3:T(8,128)} %copy.20) | data formatting | bytes 8388608 | tf_op jit(solution)/shard_map/reshape | solution.py:55
  193.2 11.7 %cholesky.286 = f32[128,128]{1,0:T(8,128)S(1)} custom-call(f32[128,128]{1,0:T(8,128)S(1)} %cholesky.426), custom_call_target="Cholesky" | custom-call | tf_op jit(solution)/shard_map/jit(cholesky)/cholesky | solution.py:34
  204.9 9.8 %custom-call.27 = f32[1,128,128]{1,2,0:T(8,128)S(1)} custom-call(f32[1,128,128]{2,1,0:T(8,128)S(1)} %get-tuple-element.61), custom_call_target="InvertDiagBlocksLowerTriangular" | custom-call | tf_op jit(solution)/shard_map/jit(cholesky)/cholesky | solution.py:34
  217.4 11.7 %cholesky.305 = f32[128,128]{1,0:T(8,128)S(1)} custom-call(f32[128,128]{1,0:T(8,128)S(1)} %cholesky.430), custom_call_target="Cholesky" | custom-call | tf_op jit(solution)/shard_map/jit(cholesky)/cholesky | solution.py:34
  229.1 10.0 %custom-call.28 = f32[1,128,128]{1,2,0:T(8,128)S(1)} custom-call(f32[1,128,128]{2,1,0:T(8,128)S(1)} %get-tuple-element.58), custom_call_target="InvertDiagBlocksLowerTriangular" | custom-call | tf_op jit(solution)/shard_map/jit(cholesky)/cholesky | solution.py:34
  240.7 11.7 %cholesky.326 = f32[128,128]{1,0:T(8,128)S(1)} custom-call(f32[128,128]{1,0:T(8,128)S(1)} %cholesky.435), custom_call_target="Cholesky" | custom-call | tf_op jit(solution)/shard_map/jit(cholesky)/cholesky | solution.py:34
  252.4 9.8 %custom-call.29 = f32[1,128,128]{1,2,0:T(8,128)S(1)} custom-call(f32[1,128,128]{2,1,0:T(8,128)S(1)} %get-tuple-element.55), custom_call_target="InvertDiagBlocksLowerTriangular" | custom-call | tf_op jit(solution)/shard_map/jit(cholesky)/cholesky | solution.py:34
  263.7 11.7 %cholesky.343 = f32[128,128]{1,0:T(8,128)S(1)} custom-call(f32[128,128]{1,0:T(8,128)S(1)} %convolution_subtract_fusion.12), custom_call_target="Cholesky" | custom-call | tf_op jit(solution)/shard_map/jit(cholesky)/cholesky | solution.py:34
  281.6 12.0 %while.4 = (s32[]{:T(128)}, f32[512,512]{1,0:T(8,128)}, s32[4,2]{0,1:T(2,128)S(1)}, f32[4,128,128]{2,1,0:T(8,128)S(1)}, s32[]{:T(128)}) while((s32[]{:T(128)}, f32[512,512]{1,0:T(8,128)}, s32[4,2]{0,1:T(2,128)S(1)}, f32[4,128,128]{2,1,0:T(8,128)S(1)}, s32[]{:T(128)}) %tuple.58), condition=%wide.while_cond, body=%wide.while_body.sunk | while | flops 2 | bytes 131181 | solution.py:30
  293.7 39.3 %custom-call.30 = f32[4,128,128]{1,2,0:T(8,128)S(1)} custom-call(f32[4,128,128]{2,1,0:T(8,128)S(1)} %get-tuple-element.18), custom_call_target="InvertDiagBlocksLowerTriangular" | custom-call | tf_op jit(solution)/shard_map/jit(_solve_triangular)/triangular_solve | solution.py:30
  349.1 11.7 %cholesky.358 = f32[128,128]{1,0:T(8,128)S(1)} custom-call(f32[128,128]{1,0:T(8,128)S(1)} %cholesky.439), custom_call_target="Cholesky" | custom-call | tf_op jit(solution)/shard_map/jit(cholesky)/cholesky | solution.py:34
  362.0 10.0 %custom-call.31 = f32[1,128,128]{1,2,0:T(8,128)S(1)} custom-call(f32[1,128,128]{2,1,0:T(8,128)S(1)} %get-tuple-element.51), custom_call_target="InvertDiagBlocksLowerTriangular" | custom-call | tf_op jit(solution)/shard_map/jit(cholesky)/cholesky | solution.py:34
  375.1 11.7 %cholesky.377 = f32[128,128]{1,0:T(8,128)S(1)} custom-call(f32[128,128]{1,0:T(8,128)S(1)} %cholesky.443), custom_call_target="Cholesky" | custom-call | tf_op jit(solution)/shard_map/jit(cholesky)/cholesky | solution.py:34
  387.5 9.8 %custom-call.32 = f32[1,128,128]{1,2,0:T(8,128)S(1)} custom-call(f32[1,128,128]{2,1,0:T(8,128)S(1)} %get-tuple-element.48), custom_call_target="InvertDiagBlocksLowerTriangular" | custom-call | tf_op jit(solution)/shard_map/jit(cholesky)/cholesky | solution.py:34
  399.7 11.7 %cholesky.398 = f32[128,128]{1,0:T(8,128)S(1)} custom-call(f32[128,128]{1,0:T(8,128)S(1)} %cholesky.448), custom_call_target="Cholesky" | custom-call | tf_op jit(solution)/shard_map/jit(cholesky)/cholesky | solution.py:34
  412.0 10.0 %custom-call.33 = f32[1,128,128]{1,2,0:T(8,128)S(1)} custom-call(f32[1,128,128]{2,1,0:T(8,128)S(1)} %get-tuple-element.45), custom_call_target="InvertDiagBlocksLowerTriangular" | custom-call | tf_op jit(solution)/shard_map/jit(cholesky)/cholesky | solution.py:34
  424.3 11.7 %cholesky.415 = f32[128,128]{1,0:T(8,128)S(1)} custom-call(f32[128,128]{1,0:T(8,128)S(1)} %convolution_subtract_fusion.11), custom_call_target="Cholesky" | custom-call | tf_op jit(solution)/shard_map/jit(cholesky)/cholesky | solution.py:34
  444.4 11.7 %while.5 = (s32[]{:T(128)}, f32[512,512]{1,0:T(8,128)}, s32[4,2]{0,1:T(2,128)S(1)}, f32[4,128,128]{2,1,0:T(8,128)S(1)}, s32[]{:T(128)}) while((s32[]{:T(128)}, f32[512,512]{1,0:T(8,128)}, s32[4,2]{0,1:T(2,128)S(1)}, f32[4,128,128]{2,1,0:T(8,128)S(1)}, s32[]{:T(128)}) %tuple.70), condition=%wide.while_cond.clone, body=%wide.while_body.clone.sunk | while | flops 2 | bytes 131181 | solution.py:30
  456.1 39.7 %custom-call.34 = f32[4,128,128]{1,2,0:T(8,128)S(1)} custom-call(f32[4,128,128]{2,1,0:T(8,128)S(1)} %get-tuple-element.19), custom_call_target="InvertDiagBlocksLowerTriangular" | custom-call | tf_op jit(solution)/shard_map/jit(_solve_triangular)/triangular_solve | solution.py:30
  504.8 4.5 fusion.46
  509.3 3.5 bitcast_subtract_fusion
  512.9 5.1 convolution_select_fusion
  517.9 4.0 copy.23
  521.9 7.2 %fusion.2 = f32[512,2048]{1,0:T(8,128)S(1)} fusion(f32[1024,2048]{1,0:T(8,128)S(1)} %bitcast.122, f32[128,512]{1,0:T(8,128)S(1)} %copy-done.8, f32[128,512]{1,0:T(8,128)S(1)} %fusion.60, f32[128,512]{1,0:T(8,128)S(1)} %fusion.62, f32[128,512]{1,0:T(8,128)S(1)} %fusion.36), kind=kOutput, calls=%fused_computation.11 | convolution fusion | flops 6443237376 | bytes 9437184 | tf_op jit(solution)/shard_map/dot_general | solution.py:13
  529.1 7.7 %fusion.106 = f32[512,2048]{1,0:T(8,128)S(1)} fusion(f32[512,512]{1,0:T(8,128)S(1)} %fusion.10, f32[512,2048]{1,0:T(8,128)S(1)} %fusion.2), kind=kOutput, calls=%fused_computation.193 | convolution fusion | flops 6442450944 | bytes 9437184 | tf_op jit(solution)/shard_map/dot_general | solution.py:17
  536.9 7.2 %fusion.7 = f32[512,2048]{1,0:T(8,128)S(1)} fusion(f32[512,2048]{1,0:T(8,128)S(1)} %fusion.106, f32[1024,2048]{1,0:T(8,128)S(1)} %bitcast.123, pred[2048]{0:T(1024)(128)(4,1)S(1)} %get-tuple-element.68, f32[128,512]{1,0:T(8,128)S(1)} %fusion.53, f32[128,512]{1,0:T(8,128)S(1)} %copy-done.6, f32[128,512]{1,0:T(8,128)S(1)} %fusion.56, f32[128,512]{1,0:T(8,128)S(1)} %fusion.34), kind=kOutput, calls=%fused_computation.16 | convolution fusion | flops 6445334528 | bytes 13633536 | tf_op jit(solution)/shard_map/dot_general | solution.py:13
  546.5 31.7 %subtract_select_fusion = f32[2048,1024]{1,0:T(8,128)} fusion(f32[2048,1024]{1,0:T(8,128)} %param.4, pred[1024]{0:T(1024)(128)(4,1)S(1)} %get-tuple-element.67, pred[2048]{0:T(1024)(128)(4,1)S(1)} %get-tuple-element.69, f32[512,1024]{1,0:T(8,128)S(1)} %copy-done.11, f32[512,1024]{1,0:T(8,128)S(1)} %copy-done.3, f32[512,2048]{1,0:T(8,128)S(1)} %fusion.7, ...), kind=kOutput, calls=%fused_computation.8 | convolution fusion | flops 25779240960 | bytes 29363200 | tf_op jit(solution)/shard_map/dot_general | solution.py:17
  (132 shorter events, 92.8 us)
Async XLA Ops:
  7.2 3.7 slice-start
  7.2 39.1 %all-gather.7.cloned.1.call-start = ((), (), s32[]{:S(2)}) async-start(), calls=%async_computation.1 | async-start | bytes 4718592 | tf_op jit(solution)/shard_map/all_gather | solution.py:59
  9.2 107.5 %all-gather.9.cloned.1.call-start = ((), (), s32[]{:S(2)}) async-start(), calls=%async_computation.2 | async-start | bytes 4227072 | tf_op jit(solution)/shard_map/all_gather | solution.py:53
  10.8 507.1 %all-gather.5.cloned.1.call-start = ((), (), s32[]{:S(2)}) async-start(), calls=%async_computation | async-start | bytes 8912896 | tf_op jit(solution)/shard_map/all_gather | solution.py:56
  192.2 1.0 copy-start.10
  333.0 6.0 %copy-start = (f32[1024,1024]{0,1:T(8,128)S(1)}, f32[1024,1024]{0,1:T(8,128)}, u32[]{:S(2)}) copy-start(f32[1024,1024]{0,1:T(8,128)} %reshape.140) | copy-start | bytes 12582916
  339.1 7.3 %copy-start.7 = (f32[128,512]{1,0:T(8,128)}, f32[128,512]{1,0:T(8,128)S(1)}, u32[]{:S(2)}) copy-start(f32[128,512]{1,0:T(8,128)S(1)} %fusion.59) | copy-start | bytes 786436
  348.1 1.0 copy-start.9
  495.8 0.7 copy-start.12
  495.8 8.9 %copy-start.4 = (f32[2,8,32,1024]{3,2,1,0:T(8,128)S(1)}, f32[2,8,32,1024]{3,2,1,0:T(8,128)}, u32[]{:S(2)}) copy-start(f32[2,8,32,1024]{3,2,1,0:T(8,128)} %copy.26) | copy-start | bytes 6291460
  500.4 8.9 %copy-start.1 = (f32[2,8,32,1024]{3,2,1,0:T(8,128)S(1)}, f32[2,8,32,1024]{3,2,1,0:T(8,128)}, u32[]{:S(2)}) copy-start(f32[2,8,32,1024]{3,2,1,0:T(8,128)} %copy.27) | copy-start | bytes 6291460
  501.8 11.1 %copy-start.5 = (f32[128,512]{1,0:T(8,128)}, f32[128,512]{1,0:T(8,128)S(1)}, u32[]{:S(2)}) copy-start(f32[128,512]{1,0:T(8,128)S(1)} %fusion.54) | copy-start | bytes 786436
  509.3 3.5 copy-start.2
  517.9 4.0 copy-start.8
  529.1 7.8 %copy-start.6 = (f32[128,512]{1,0:T(8,128)S(1)}, f32[128,512]{1,0:T(8,128)}, u32[]{:S(2)}) copy-start(f32[128,512]{1,0:T(8,128)} %copy-done.5) | copy-start | bytes 786436
  544.0 1.8 copy-start.3
  544.1 2.4 copy-start.11
Sparse Core Ops, SparseCore 0:
  10.3 35.9 all-gather.6
  50.0 66.6 all-gather.8
  118.9 67.6 all-gather.4
where the time goes:
time: 592 us; the launch traced here: 585 us
  other arithmetic  260 us (44%)
  local copies, waits for them, and re-layouts  106 us (18%)
  matrix products  99.3 us (17%)
  waiting for transfers between devices  99.1 us (17%)
  between operations  19.9 us (3%)
    another operation x29, other arithmetic, sym_chol(): return jnp.linalg.cholesky(block)  160 us
    another operation x5, other arithmetic, tri_inverse(): return jax.scipy.linalg.solve_triangular(lower, eye, lower=True)  82.9 us
    all_gather x1, waiting for transfers between devices, local(): blocks = lax.all_gather(corner, ('row', 'col'), axis=0, tiled=True)  65 us
    dot_general x4, matrix products, mm_tn(): lax.dot_general(a, b, (((0,), (0,)), ((), ())), precision=HIGHEST, prefer...  45.8 us
    all_gather x1, waiting for transfers between devices, local(): rows_part = lax.all_gather(kernel[:lead_r, :], 'row', axis=0, tiled=True)  34.1 us
    transpose x1, local copies, waits for them, and re-layouts, local(): a_lead = blocks.transpose(2, 0, 3, 4, 1, 5).reshape(lead, lead)  26.1 us
    dot_general x5, matrix products, mm(): return jnp.dot(a, b, precision=HIGHEST, preferred_element_type=jnp.float32)  25.8 us
    another operation x27, local copies, waits for them, and re-layouts, tri_inverse(): return jax.scipy.linalg.solve_triangular(lower, eye, lower=True)  23.6 us
  transfers between devices with their start and end apart: 3, of which 2 were waited for; matrix products, arithmetic and copies ran while one was open for 69% of the time, Pallas kernels for 0%

commit v1 on v0

--- a/solution.py
+++ b/solution.py
@@ -7,6 +7,27 @@
 PANELS = 2
 TILE = 32
 HIGHEST = lax.Precision.HIGHEST
+
+
+def collect(x, axis, dim):
+    peers, here, width = (lax.axis_size(axis), lax.axis_index(axis), x.shape[dim])
+    right = [(i, (i + 1) % peers) for i in range(peers)]
+    downward = [(i, (i - 1) % peers) for i in range(peers)]
+    filled = jnp.zeros((*x.shape[:dim], peers * width, *x.shape[dim + 1 :]), x.dtype)
+    filled = lax.dynamic_update_slice_in_dim(filled, x, here * width, axis=dim)
+    from_left = from_right = x
+    half = peers // 2
+    for turn in range(1, half + 1):
+        from_left = lax.ppermute(from_left, axis, right)
+        filled = lax.dynamic_update_slice_in_dim(
+            filled, from_left, (here - turn) % peers * width, axis=dim
+        )
+        if turn < peers - half:
+            from_right = lax.ppermute(from_right, axis, downward)
+            filled = lax.dynamic_update_slice_in_dim(
+                filled, from_right, (here + turn) % peers * width, axis=dim
+            )
+    return filled
 
 
 def mm(a, b):
@@ -56,7 +77,7 @@
     cols_part = lax.all_gather(kernel[:, :lead_c], "col", axis=1, tiled=True)
     cols_part = cols_part.reshape(rows_loc, grid_cols, lead_ct, TILE)
     x_rows = cols_part.transpose(0, 2, 1, 3).reshape(rows_loc, lead)
-    rows_part = lax.all_gather(kernel[:lead_r, :], "row", axis=0, tiled=True)
+    rows_part = collect(kernel[:lead_r, :], "row", 0)
     rows_part = rows_part.reshape(grid_rows, lead_rt, TILE, cols_loc)
     y_cols = rows_part.transpose(1, 0, 2, 3).reshape(lead, cols_loc)
     a00 = a_lead[:PANEL, :PANEL]

time: 592 us -> 558 us (0.943)
  waiting for transfers between devices: 99.1 us -> 41.5 us
  starting transfers between devices: 0.12 us -> 12.3 us
  local copies, waits for them, and re-layouts: 106 us -> 117 us
    all_gather x1, waiting for transfers between devices: 65 us -> 25.8 us  [local(): blocks = lax.all_gather(corner, ('row', 'col'), axis=0, tiled=True)]
    all_gather x1 -> x0, waiting for transfers between devices: 34.1 us -> none  [local(): rows_part = lax.all_gather(kernel[:lead_r, :], 'row', axis=0, tiled=True)]
    ppermute x0 -> x7, waiting for transfers between devices: none -> 15.7 us  [the longest x4 15.6 us: collect(): from_left = lax.ppermute(from_left, axis, right)]
    ppermute x0 -> x7, starting transfers between devices: none -> 12.2 us  [the longest x4 10.5 us: collect(): from_left = lax.ppermute(from_left, axis, right)]
    dynamic_update_slice x0 -> x7, local copies, waits for them, and re-layouts: none -> 7.91 us  [the longest x4 5.43 us: collect(): lax.dynamic_update_slice_in_dim(filled, from_left, (here - turn) % peers...]
  transfers between devices with their start and end apart: 3 -> 9, of which waited for: 2 -> 6; matrix products, arithmetic and copies ran while one was open for 69% -> 75% of each run, Pallas kernels for 0% -> 0%
where the time goes in v1:
time: 558 us; the launch traced here: 550 us
  other arithmetic  260 us (47%)
  local copies, waits for them, and re-layouts  117 us (21%)
  matrix products  99.4 us (18%)
  waiting for transfers between devices  41.5 us (7%)
  between operations  20.2 us (4%)
  starting transfers between devices  12.3 us (2%)
    another operation x29, other arithmetic, sym_chol(): return jnp.linalg.cholesky(block)  160 us
    another operation x5, other arithmetic, tri_inverse(): return jax.scipy.linalg.solve_triangular(lower, eye, lower=True)  82.9 us
    dot_general x4, matrix products, mm_tn(): lax.dot_general(a, b, (((0,), (0,)), ((), ())), precision=HIGHEST, prefer...  45.8 us
    transpose x1, local copies, waits for them, and re-layouts, local(): a_lead = blocks.transpose(2, 0, 3, 4, 1, 5).reshape(lead, lead)  26.1 us
    all_gather x1, waiting for transfers between devices, local(): blocks = lax.all_gather(corner, ('row', 'col'), axis=0, tiled=True)  25.8 us
    dot_general x5, matrix products, mm(): return jnp.dot(a, b, precision=HIGHEST, preferred_element_type=jnp.float32)  25.8 us
    another operation x27, local copies, waits for them, and re-layouts, tri_inverse(): return jax.scipy.linalg.solve_triangular(lower, eye, lower=True)  23.6 us
    reshape x1, local copies, waits for them, and re-layouts, local(): blocks = blocks.reshape(grid_rows, grid_cols, lead_rt, TILE, lead_ct, TILE)  16.6 us
  transfers between devices with their start and end apart: 9, of which 6 were waited for; matrix products, arithmetic and copies ran while one was open for 75% of the time, Pallas kernels for 0%

profile of v1, /device:TPU:1, one launch (start us, length us, event | category | flops | bytes accessed | tf_op | source)
XLA Modules:
  0.0 550.3 jit_solution(8823926093509423216)
XLA Ops:
  16.4 6.1 %collective-permute-done = f32[128,1024]{1,0:T(8,128)S(1)} collective-permute-done((f32[128,1024]{1,0:T(8,128)S(1)}, f32[128,1024]{1,0:T(8,128)S(1)}, u32[]{:S(2)}, u32[]{:S(2)}) %collective-permute-start) | collective-permute-done | bytes 524320 | tf_op jit(solution)/shard_map/ppermute | solution.py:21
  26.4 4.9 collective-permute-done.2
  56.0 25.8 %all-gather.6.cloned.1.call-done = f32[128,1,8192]{2,1,0:T(1,128)} async-done(((f32[1,1,8192]{2,1,0:T(1,128)}), f32[128,1,8192]{2,1,0:T(1,128)}) %all-gather.6.cloned.1.call-update) | async-done | bytes 4194320 | tf_op jit(solution)/shard_map/all_gather | solution.py:74
  81.8 13.2 %reduce.16 = f32[128,8192]{1,0:T(8,128)} reduce(f32[128,1,8192]{2,1,0:T(1,128)} %all-gather.6.cloned.1.call-done, f32[]{:T(128)} %constant.262), dimensions={1}, to_apply=%all-gather.reduce_sub_computation | reduce | bytes 8388612 | tf_op jit(solution)/shard_map/all_gather | solution.py:74
  95.0 16.6 %reshape.139 = f32[8,16,4,32,2,32]{5,4,3,2,1,0:T(2,128)} reshape(f32[128,8192]{1,0:T(8,128)} %reduce.16) | data formatting | bytes 8388608 | tf_op jit(solution)/shard_map/reshape | solution.py:75
  111.6 26.1 %copy.20 = f32[4,8,32,2,16,32]{2,1,0,5,4,3:T(8,128)} copy(f32[4,8,32,2,16,32]{5,3,2,0,4,1:T(2,128)} %bitcast.121) | data formatting | bytes 8388608 | tf_op jit(solution)/shard_map/transpose | solution.py:76
  137.6 14.3 %reshape.140 = f32[1024,1024]{0,1:T(8,128)} reshape(f32[4,8,32,2,16,32]{2,1,0,5,4,3:T(8,128)} %copy.20) | data formatting | bytes 8388608 | tf_op jit(solution)/shard_map/reshape | solution.py:76
  158.2 11.7 %cholesky.286 = f32[128,128]{1,0:T(8,128)S(1)} custom-call(f32[128,128]{1,0:T(8,128)S(1)} %cholesky.426), custom_call_target="Cholesky" | custom-call | tf_op jit(solution)/shard_map/jit(cholesky)/cholesky | solution.py:55
  170.0 9.8 %custom-call.27 = f32[1,128,128]{1,2,0:T(8,128)S(1)} custom-call(f32[1,128,128]{2,1,0:T(8,128)S(1)} %get-tuple-element.63), custom_call_target="InvertDiagBlocksLowerTriangular" | custom-call | tf_op jit(solution)/shard_map/jit(cholesky)/cholesky | solution.py:55
  182.4 11.7 %cholesky.305 = f32[128,128]{1,0:T(8,128)S(1)} custom-call(f32[128,128]{1,0:T(8,128)S(1)} %cholesky.430), custom_call_target="Cholesky" | custom-call | tf_op jit(solution)/shard_map/jit(cholesky)/cholesky | solution.py:55
  194.2 10.0 %custom-call.28 = f32[1,128,128]{1,2,0:T(8,128)S(1)} custom-call(f32[1,128,128]{2,1,0:T(8,128)S(1)} %get-tuple-element.60), custom_call_target="InvertDiagBlocksLowerTriangular" | custom-call | tf_op jit(solution)/shard_map/jit(cholesky)/cholesky | solution.py:55
  205.7 11.7 %cholesky.326 = f32[128,128]{1,0:T(8,128)S(1)} custom-call(f32[128,128]{1,0:T(8,128)S(1)} %cholesky.435), custom_call_target="Cholesky" | custom-call | tf_op jit(solution)/shard_map/jit(cholesky)/cholesky | solution.py:55
  217.5 9.8 %custom-call.29 = f32[1,128,128]{1,2,0:T(8,128)S(1)} custom-call(f32[1,128,128]{2,1,0:T(8,128)S(1)} %get-tuple-element.57), custom_call_target="InvertDiagBlocksLowerTriangular" | custom-call | tf_op jit(solution)/shard_map/jit(cholesky)/cholesky | solution.py:55
  228.7 11.7 %cholesky.343 = f32[128,128]{1,0:T(8,128)S(1)} custom-call(f32[128,128]{1,0:T(8,128)S(1)} %convolution_subtract_fusion.12), custom_call_target="Cholesky" | custom-call | tf_op jit(solution)/shard_map/jit(cholesky)/cholesky | solution.py:55
  246.7 12.0 %while.4 = (s32[]{:T(128)}, f32[512,512]{1,0:T(8,128)}, s32[4,2]{0,1:T(2,128)S(1)}, f32[4,128,128]{2,1,0:T(8,128)S(1)}, s32[]{:T(128)}) while((s32[]{:T(128)}, f32[512,512]{1,0:T(8,128)}, s32[4,2]{0,1:T(2,128)S(1)}, f32[4,128,128]{2,1,0:T(8,128)S(1)}, s32[]{:T(128)}) %tuple.59), condition=%wide.while_cond, body=%wide.while_body.sunk | while | flops 2 | bytes 131181 | solution.py:51
  258.7 39.3 %custom-call.30 = f32[4,128,128]{1,2,0:T(8,128)S(1)} custom-call(f32[4,128,128]{2,1,0:T(8,128)S(1)} %get-tuple-element.18), custom_call_target="InvertDiagBlocksLowerTriangular" | custom-call | tf_op jit(solution)/shard_map/jit(_solve_triangular)/triangular_solve | solution.py:51
  314.2 11.7 %cholesky.358 = f32[128,128]{1,0:T(8,128)S(1)} custom-call(f32[128,128]{1,0:T(8,128)S(1)} %cholesky.439), custom_call_target="Cholesky" | custom-call | tf_op jit(solution)/shard_map/jit(cholesky)/cholesky | solution.py:55
  327.0 10.0 %custom-call.31 = f32[1,128,128]{1,2,0:T(8,128)S(1)} custom-call(f32[1,128,128]{2,1,0:T(8,128)S(1)} %get-tuple-element.53), custom_call_target="InvertDiagBlocksLowerTriangular" | custom-call | tf_op jit(solution)/shard_map/jit(cholesky)/cholesky | solution.py:55
  340.2 11.7 %cholesky.377 = f32[128,128]{1,0:T(8,128)S(1)} custom-call(f32[128,128]{1,0:T(8,128)S(1)} %cholesky.443), custom_call_target="Cholesky" | custom-call | tf_op jit(solution)/shard_map/jit(cholesky)/cholesky | solution.py:55
  352.5 9.8 %custom-call.32 = f32[1,128,128]{1,2,0:T(8,128)S(1)} custom-call(f32[1,128,128]{2,1,0:T(8,128)S(1)} %get-tuple-element.50), custom_call_target="InvertDiagBlocksLowerTriangular" | custom-call | tf_op jit(solution)/shard_map/jit(cholesky)/cholesky | solution.py:55
  364.7 11.7 %cholesky.398 = f32[128,128]{1,0:T(8,128)S(1)} custom-call(f32[128,128]{1,0:T(8,128)S(1)} %cholesky.448), custom_call_target="Cholesky" | custom-call | tf_op jit(solution)/shard_map/jit(cholesky)/cholesky | solution.py:55
  377.1 10.0 %custom-call.33 = f32[1,128,128]{1,2,0:T(8,128)S(1)} custom-call(f32[1,128,128]{2,1,0:T(8,128)S(1)} %get-tuple-element.47), custom_call_target="InvertDiagBlocksLowerTriangular" | custom-call | tf_op jit(solution)/shard_map/jit(cholesky)/cholesky | solution.py:55
  389.3 11.7 %cholesky.415 = f32[128,128]{1,0:T(8,128)S(1)} custom-call(f32[128,128]{1,0:T(8,128)S(1)} %convolution_subtract_fusion.11), custom_call_target="Cholesky" | custom-call | tf_op jit(solution)/shard_map/jit(cholesky)/cholesky | solution.py:55
  409.4 11.7 %while.5 = (s32[]{:T(128)}, f32[512,512]{1,0:T(8,128)}, s32[4,2]{0,1:T(2,128)S(1)}, f32[4,128,128]{2,1,0:T(8,128)S(1)}, s32[]{:T(128)}) while((s32[]{:T(128)}, f32[512,512]{1,0:T(8,128)}, s32[4,2]{0,1:T(2,128)S(1)}, f32[4,128,128]{2,1,0:T(8,128)S(1)}, s32[]{:T(128)}) %tuple.69), condition=%wide.while_cond.clone, body=%wide.while_body.clone.sunk | while | flops 2 | bytes 131181 | solution.py:51
  421.1 39.7 %custom-call.34 = f32[4,128,128]{1,2,0:T(8,128)S(1)} custom-call(f32[4,128,128]{2,1,0:T(8,128)S(1)} %get-tuple-element.19), custom_call_target="InvertDiagBlocksLowerTriangular" | custom-call | tf_op jit(solution)/shard_map/jit(_solve_triangular)/triangular_solve | solution.py:51
  469.8 4.5 fusion.46
  477.9 5.1 convolution_select_fusion
  483.0 4.0 copy.23
  487.0 7.2 %fusion.2 = f32[512,2048]{1,0:T(8,128)S(1)} fusion(f32[1024,2048]{1,0:T(8,128)S(1)} %bitcast.122, f32[128,512]{1,0:T(8,128)S(1)} %copy-done.8, f32[128,512]{1,0:T(8,128)S(1)} %fusion.60, f32[128,512]{1,0:T(8,128)S(1)} %fusion.62, f32[128,512]{1,0:T(8,128)S(1)} %fusion.36), kind=kOutput, calls=%fused_computation.11 | convolution fusion | flops 6443237376 | bytes 9437184 | tf_op jit(solution)/shard_map/dot_general | solution.py:34
  494.2 7.7 %fusion.107 = f32[512,2048]{1,0:T(8,128)S(1)} fusion(f32[512,512]{1,0:T(8,128)S(1)} %fusion.10, f32[512,2048]{1,0:T(8,128)S(1)} %fusion.2), kind=kOutput, calls=%fused_computation.202 | convolution fusion | flops 6442450944 | bytes 9437184 | tf_op jit(solution)/shard_map/dot_general | solution.py:38
  501.9 7.2 %fusion.7 = f32[512,2048]{1,0:T(8,128)S(1)} fusion(f32[512,2048]{1,0:T(8,128)S(1)} %fusion.107, f32[1024,2048]{1,0:T(8,128)S(1)} %bitcast.123, pred[2048]{0:T(1024)(128)(4,1)S(1)} %get-tuple-element.70, f32[128,512]{1,0:T(8,128)S(1)} %fusion.53, f32[128,512]{1,0:T(8,128)S(1)} %copy-done.6, f32[128,512]{1,0:T(8,128)S(1)} %fusion.56, f32[128,512]{1,0:T(8,128)S(1)} %fusion.34), kind=kOutput, calls=%fused_computation.16 | convolution fusion | flops 6445334528 | bytes 13633536 | tf_op jit(solution)/shard_map/dot_general | solution.py:34
  511.5 31.7 %subtract_select_fusion = f32[2048,1024]{1,0:T(8,128)} fusion(f32[2048,1024]{1,0:T(8,128)} %param.4, pred[1024]{0:T(1024)(128)(4,1)S(1)} %get-tuple-element.69, pred[2048]{0:T(1024)(128)(4,1)S(1)} %get-tuple-element.71, f32[512,1024]{1,0:T(8,128)S(1)} %copy-done.11, f32[512,1024]{1,0:T(8,128)S(1)} %copy-done.3, f32[512,2048]{1,0:T(8,128)S(1)} %fusion.7, ...), kind=kOutput, calls=%fused_computation.8 | convolution fusion | flops 25779240960 | bytes 29363200 | tf_op jit(solution)/shard_map/dot_general | solution.py:38
  (153 shorter events, 123.6 us)
Async XLA Ops:
  7.2 18.1 %slice-start = ((f32[2048,1024]{1,0:T(8,128)}), f32[2048,64]{1,0:T(8,128)S(1)}, s32[]{:S(2)}) async-start(f32[2048,1024]{1,0:T(8,128)} %param.4), calls=%async_computation.2 | async-start | bytes 2097152 | tf_op jit(solution)/shard_map/slice | solution.py:77
  7.2 74.6 %all-gather.6.cloned.1.call-start = ((), (), s32[]{:S(2)}) async-start(), calls=%async_computation.1 | async-start | bytes 4227072 | tf_op jit(solution)/shard_map/all_gather | solution.py:74
  8.9 474.1 %all-gather.4.cloned.1.call-start = ((), (), s32[]{:S(2)}) async-start(), calls=%async_computation | async-start | bytes 8912896 | tf_op jit(solution)/shard_map/all_gather | solution.py:77
  13.4 9.2 %collective-permute-start = (f32[128,1024]{1,0:T(8,128)S(1)}, f32[128,1024]{1,0:T(8,128)S(1)}, u32[]{:S(2)}, u32[]{:S(2)}) collective-permute-start(f32[128,1024]{1,0:T(8,128)S(1)} %get-tuple-element.40), channel_id=1, source_target_pairs={{0,16},{16,32},{32,48},{48,64},{64,80},{80,96},{96,112},{112,0},{1... | collective-permute-start | bytes 1572872 | tf_op jit(solution)/shard_map/ppermute | solution.py:21
  16.4 8.6 %collective-permute-start.1 = (f32[128,1024]{1,0:T(8,128)S(1)}, f32[128,1024]{1,0:T(8,128)S(1)}, u32[]{:S(2)}, u32[]{:S(2)}) collective-permute-start(f32[128,1024]{1,0:T(8,128)S(1)} %get-tuple-element.40), channel_id=1, source_target_pairs={{0,112},{16,0},{32,16},{48,32},{64,48},{80,64},{96,80},{112,96},{1... | collective-permute-start | bytes 1572872 | tf_op jit(solution)/shard_map/ppermute | solution.py:26
  22.5 11.4 %copy-start.12 = (f32[128,1024]{1,0:T(8,128)}, f32[128,1024]{1,0:T(8,128)S(1)}, u32[]{:S(2)}) copy-start(f32[128,1024]{1,0:T(8,128)S(1)} %collective-permute-done) | copy-start | bytes 1572868
  22.5 8.8 %collective-permute-start.2 = (f32[128,1024]{1,0:T(8,128)S(1)}, f32[128,1024]{1,0:T(8,128)}, u32[]{:S(2)}, u32[]{:S(2)}) collective-permute-start(f32[128,1024]{1,0:T(8,128)S(1)} %collective-permute-done), channel_id=1, source_target_pairs={{0,16},{16,32},{32,48},{48,64},{64,80},{80,96},{96,112},{112,0},{1... | collective-permute-start | bytes 1572872 | tf_op jit(solution)/shard_map/ppermute | solution.py:21
  25.0 9.2 %collective-permute-start.3 = (f32[128,1024]{1,0:T(8,128)S(1)}, f32[128,1024]{1,0:T(8,128)S(1)}, u32[]{:S(2)}, u32[]{:S(2)}) collective-permute-start(f32[128,1024]{1,0:T(8,128)S(1)} %collective-permute-done.1), channel_id=1, source_target_pairs={{0,112},{16,0},{32,16},{48,32},{64,48},{80,64},{96,80},{112,96},{1... | collective-permute-start | bytes 1572872 | tf_op jit(solution)/shard_map/ppermute | solution.py:26
  31.3 9.1 %collective-permute-start.4 = (f32[128,1024]{1,0:T(8,128)}, f32[128,1024]{1,0:T(8,128)S(1)}, u32[]{:S(2)}, u32[]{:S(2)}) collective-permute-start(f32[128,1024]{1,0:T(8,128)} %collective-permute-done.2), channel_id=1, source_target_pairs={{0,16},{16,32},{32,48},{48,64},{64,80},{80,96},{96,112},{112,0},{1... | collective-permute-start | bytes 1572872 | tf_op jit(solution)/shard_map/ppermute | solution.py:21
  34.2 13.0 %collective-permute-start.5 = (f32[128,1024]{1,0:T(8,128)S(1)}, f32[128,1024]{1,0:T(8,128)S(1)}, u32[]{:S(2)}, u32[]{:S(2)}) collective-permute-start(f32[128,1024]{1,0:T(8,128)S(1)} %collective-permute-done.3), channel_id=1, source_target_pairs={{0,112},{16,0},{32,16},{48,32},{64,48},{80,64},{96,80},{112,96},{1... | collective-permute-start | bytes 1572872 | tf_op jit(solution)/shard_map/ppermute | solution.py:26
  40.4 9.2 %collective-permute-start.6 = (f32[128,1024]{1,0:T(8,128)S(1)}, f32[128,1024]{1,0:T(8,128)S(1)}, u32[]{:S(2)}, u32[]{:S(2)}) collective-permute-start(f32[128,1024]{1,0:T(8,128)S(1)} %collective-permute-done.4), channel_id=1, source_target_pairs={{0,16},{16,32},{32,48},{48,64},{64,80},{80,96},{96,112},{112,0},{1... | collective-permute-start | bytes 1572872 | tf_op jit(solution)/shard_map/ppermute | solution.py:21
  157.2 1.0 copy-start.10
  298.0 6.1 %copy-start = (f32[1024,1024]{0,1:T(8,128)S(1)}, f32[1024,1024]{0,1:T(8,128)}, u32[]{:S(2)}) copy-start(f32[1024,1024]{0,1:T(8,128)} %reshape.140) | copy-start | bytes 12582916
  304.1 7.3 %copy-start.7 = (f32[128,512]{1,0:T(8,128)}, f32[128,512]{1,0:T(8,128)S(1)}, u32[]{:S(2)}) copy-start(f32[128,512]{1,0:T(8,128)S(1)} %fusion.59) | copy-start | bytes 786436
  313.2 1.0 copy-start.9
  460.9 0.7 copy-start.13
  460.9 8.9 %copy-start.4 = (f32[2,8,32,1024]{3,2,1,0:T(8,128)S(1)}, f32[2,8,32,1024]{3,2,1,0:T(8,128)}, u32[]{:S(2)}) copy-start(f32[2,8,32,1024]{3,2,1,0:T(8,128)} %copy.26) | copy-start | bytes 6291460
  465.4 8.9 %copy-start.1 = (f32[2,8,32,1024]{3,2,1,0:T(8,128)S(1)}, f32[2,8,32,1024]{3,2,1,0:T(8,128)}, u32[]{:S(2)}) copy-start(f32[2,8,32,1024]{3,2,1,0:T(8,128)} %copy.27) | copy-start | bytes 6291460
  466.9 11.1 %copy-start.5 = (f32[128,512]{1,0:T(8,128)}, f32[128,512]{1,0:T(8,128)S(1)}, u32[]{:S(2)}) copy-start(f32[128,512]{1,0:T(8,128)S(1)} %fusion.54) | copy-start | bytes 786436
  474.3 3.5 copy-start.2
  483.0 4.0 copy-start.8
  494.2 7.8 %copy-start.6 = (f32[128,512]{1,0:T(8,128)S(1)}, f32[128,512]{1,0:T(8,128)}, u32[]{:S(2)}) copy-start(f32[128,512]{1,0:T(8,128)} %copy-done.5) | copy-start | bytes 786436
  509.1 1.8 copy-start.3
  509.1 2.4 copy-start.11
Sparse Core Ops, SparseCore 0:
  11.1 70.5 all-gather.5
  83.9 67.6 all-gather.3
